TPU v7x, 256 devices: a whole 4x4x8 slice. The times are simulated.
256 devices in a mesh: dp: 2 (over core), seq: 16 (over x, y), tensor: 8 (over z).
Axes of the slice: x: 4, y: 4, z: 8, core: 2. Of those that a mesh axis runs over, the one named last changes fastest.
Arguments:
- hidden: bfloat16 [16384, 7168], P(('dp', 'seq')), may hold values from -34 to 34
- grad_out: bfloat16 [16384, 4096], P(('dp', 'seq'), 'tensor'), may hold values from -24 to 24
- master_weight: float32 [7168, 4096], P(('dp', 'seq'), 'tensor'), may hold values from -6 to 6
- row_prev: float32 [7168], P(('dp', 'seq')), may hold values from 0.01 to 0.3
- col_prev: float32 [4096], P('tensor'), may hold values from 0.01 to 0.3
Outputs:
- new_weight: bfloat16 [7168, 4096], P('dp', 'tensor')
- update: float32 [7168, 4096], P(('dp', 'seq'), 'tensor')
- new_rows: float32 [7168], P(('dp', 'seq'))
- new_cols: float32 [4096], P('tensor')
All inputs are finite; a program needn't handle non-finite values.
Results may differ from a plain program's by a relative error of at most 0.0004.
Values may be sent and summed in bfloat16 or wider, within the bound.
A program may use at most 128 MiB of HBM per device.

v0:
```python
import jax
import jax.numpy as jnp
from jax import lax
from jax.sharding import PartitionSpec as P

D = 4096
FF_WIN = 7168


decay_rate = 0.8
learn_rate = 0.05
small_term = 1e-06


def per_device(hidden, grad_out, master_weight, row_prev, col_prev):
    grads = lax.psum_scatter(
        lax.dot_general(
            hidden, grad_out, (((0,), (0,)), ((), ())), preferred_element_type=jnp.float32
        ),
        ("dp", "seq"),
        scatter_dimension=0,
        tiled=True,
    )
    squares = grads * grads + small_term
    col_total = lax.psum(jnp.sum(squares, axis=0), ("dp", "seq"))
    row_total = lax.psum(jnp.sum(squares, axis=1), "tensor")
    new_rows = decay_rate * row_prev + (1.0 - decay_rate) * row_total / D
    new_cols = decay_rate * col_prev + (1.0 - decay_rate) * col_total / FF_WIN
    second = new_rows[:, None] * new_cols[None, :]
    raw = grads / jnp.sqrt(second)
    raw_total = lax.psum(jnp.sum(raw * raw), ("dp", "seq", "tensor"))
    size = jnp.sqrt(raw_total / (FF_WIN * D))
    update = raw / jnp.maximum(1.0, size)
    fresh = (master_weight - learn_rate * update).astype(jnp.bfloat16)
    new_weight = lax.all_gather(fresh, "seq", axis=0, tiled=True)
    return (new_weight, update, new_rows, new_cols)


def solution(mesh):
    return jax.shard_map(
        per_device,
        mesh=mesh,
        in_specs=(
            P(("dp", "seq"), None),
            P(("dp", "seq"), "tensor"),
            P(("dp", "seq"), "tensor"),
            P(("dp", "seq")),
            P("tensor"),
        ),
        out_specs=(P("dp", "tensor"), P(("dp", "seq"), "tensor"), P(("dp", "seq")), P("tensor")),
        check_vma=False,
    )
```

profile of v0, /device:TPU:2, one launch (start us, length us, event | category | flops | bytes accessed | tf_op | source)
XLA Modules:
  0.0 361.4 jit_solution(1551394529505662)
XLA Ops:
  7.2 0.0 copy-start
  7.2 0.0 reduce-scatter.2.cloned.1.call-start
  7.2 1.0 copy-done
  8.2 10.5 %fusion.4 = f32[7168,512]{1,0:T(8,128)} fusion(bf16[512,7168]{1,0:T(8,128)(2,1)} %param.5, bf16[512,512]{1,0:T(8,128)(2,1)S(1)} %copy-done), kind=kOutput, calls=%fused_computation.9 | convolution fusion | flops 3758096384 | bytes 22544384 | tf_op jit(solution)/shard_map/dot_general | solution.py:17
  18.7 0.0 copy-start.5
  18.7 0.0 reduce-scatter.2.cloned.1.call-update
  18.7 0.0 all-gather.2.cloned.1.call-start
  18.8 120.3 %reduce-scatter.2.cloned.1.call-done = f32[224,512]{1,0:T(8,128)} async-done(((f32[7168,512]{1,0:T(8,128)}), f32[224,512]{1,0:T(8,128)}) %reduce-scatter.2.cloned.1.call-update) | async-done | bytes 458768 | tf_op jit(solution)/shard_map/reduce_scatter | solution.py:16
  139.1 1.2 fusion.1
  140.3 17.5 %psum.21 = f32[224]{0:T(256)S(1)} all-reduce(f32[224]{0:T(256)S(1)} %get-tuple-element.4), channel_id=1, replica_groups=mesh['dp'=2,'seq'=16,'tensor'=8] {'tensor'}, use_global_device_ids=true, to_apply=%region_2.0 | all-reduce | flops 224 | bytes 1792 | tf_op jit(solution)/shard_map/psum | solution.py:26
  157.7 62.6 %psum.22 = f32[512]{0:T(512)S(1)} all-reduce(f32[512]{0:T(512)S(1)} %get-tuple-element.5), channel_id=1, replica_groups=mesh['dp'=2,'seq'=16,'tensor'=8] {'dp','seq'}, use_global_device_ids=true, to_apply=%region_4.0 | all-reduce | flops 512 | bytes 4096 | tf_op jit(solution)/shard_map/psum | solution.py:25
  220.3 0.0 copy-done.5
  220.3 0.0 copy-done.4
  220.4 0.0 copy-start.3
  220.4 0.0 copy-start.2
  220.4 1.8 multiply_reduce_fusion
  222.2 74.1 %psum.23 = f32[]{:T(128)} all-reduce(f32[]{:T(128)} %multiply_reduce_fusion), channel_id=1, replica_groups=mesh['dp'=2,'seq'=16,'tensor'=8] {'dp','seq','tensor'}, use_global_device_ids=true, to_apply=%region_6.0 | all-reduce | flops 1 | bytes 8 | tf_op jit(solution)/shard_map/psum | solution.py:31
  297.0 0.0 copy-done.1
  297.1 2.0 subtract_convert_fusion
  299.1 0.0 all-gather.2.cloned.1.call-update
  299.1 51.3 %all-gather.2.cloned.1.call-done = bf16[3584,512]{1,0:T(8,128)(2,1)} async-done(((bf16[224,512]{1,0:T(8,128)(2,1)}), bf16[3584,512]{1,0:T(8,128)(2,1)}) %all-gather.2.cloned.1.call-update) | async-done | bytes 3670032 | tf_op jit(solution)/shard_map/all_gather | solution.py:35
  350.4 4.1 %copy.10 = bf16[3584,512]{1,0:T(8,128)(2,1)} copy(bf16[3584,512]{1,0:T(8,128)(2,1)} %all-gather.2.cloned.1.call-done) | data formatting | bytes 7340032
  354.6 0.0 copy-done.3
  354.6 0.0 copy-done.2
  (4 shorter events, 0.0 us)
Async XLA Ops:
  7.2 1.0 copy-start
  7.2 131.9 %reduce-scatter.2.cloned.1.call-start = ((), (), s32[]{:S(2)}) async-start(), calls=%async_computation.1 | async-start | bytes 15138816 | tf_op jit(solution)/shard_map/reduce_scatter | solution.py:16
  18.7 201.6 %copy-start.5 = (f32[224]{0:T(256)S(1)}, f32[224]{0:T(256)}, u32[]{:S(2)}) copy-start(f32[224]{0:T(256)} %param.8) | copy-start | bytes 2692
  18.7 201.7 %copy-start.4 = (f32[512]{0:T(512)S(1)}, f32[512]{0:T(512)}, u32[]{:S(2)}) copy-start(f32[512]{0:T(512)} %param.9) | copy-start | bytes 6148
  18.7 278.4 %copy-start.1 = (f32[224,512]{1,0:T(8,128)S(1)}, f32[224,512]{1,0:T(8,128)}, u32[]{:S(2)}) copy-start(f32[224,512]{1,0:T(8,128)} %param.7) | copy-start | bytes 1376260
  18.7 331.7 %all-gather.2.cloned.1.call-start = ((), (), s32[]{:S(2)}) async-start(), calls=%async_computation.2 | async-start | bytes 3899392 | tf_op jit(solution)/shard_map/all_gather | solution.py:35
  220.4 134.2 %copy-start.3 = (f32[224]{0:T(256)}, f32[224]{0:T(256)S(1)}, u32[]{:S(2)}) copy-start(f32[224]{0:T(256)S(1)} %multiply_add_fusion.2) | copy-start | bytes 2692
  220.4 134.2 %copy-start.2 = (f32[512]{0:T(512)}, f32[512]{0:T(512)S(1)}, u32[]{:S(2)}) copy-start(f32[512]{0:T(512)S(1)} %multiply_add_fusion.1) | copy-start | bytes 6148
Sparse Core Ops, SparseCore 0:
  18.8 120.1 reduce-scatter.1
  299.2 51.1 all-gather.1
where the time goes:
time: 363 us; the launch traced here: 361 us
  waiting for transfers between devices  172 us (47%)
  blocking collectives  154 us (42%)
  between operations  14.8 us (4%)
  matrix products  10.5 us (3%)
  local copies, waits for them, and re-layouts  5.13 us (1%)
  other arithmetic  5.03 us (1%)
    reduce_scatter x1, waiting for transfers between devices, per_device(): lax.psum_scatter(lax.dot_general(hidden, grad_out, (((0,), (0,)), ((), ()...  120 us
    psum x1, blocking collectives, per_device(): raw_total = lax.psum(jnp.sum(raw * raw), ('dp', 'seq', 'tensor'))  74.1 us
    psum x1, blocking collectives, per_device(): col_total = lax.psum(jnp.sum(squares, axis=0), ('dp', 'seq'))  62.6 us
    all_gather x1, waiting for transfers between devices, per_device(): new_weight = lax.all_gather(fresh, 'seq', axis=0, tiled=True)  51.3 us
    psum x1, blocking collectives, per_device(): row_total = lax.psum(jnp.sum(squares, axis=1), 'tensor')  17.5 us
    dot_general x1, matrix products, per_device(): lax.dot_general(hidden, grad_out, (((0,), (0,)), ((), ())), preferred_ele...  10.5 us
  transfers between devices with their start and end apart: 2, of which 2 were waited for; matrix products, arithmetic and copies ran while one was open for 0% of the time, Pallas kernels for 0%

commit v1 on v0

v1 whole, which is shorter than its diff:
```python
import jax
import jax.numpy as jnp
from jax import lax
from jax.experimental import pallas as pl
from jax.experimental.pallas import tpu as pltpu
from jax.sharding import PartitionSpec as P

D = 4096
FF_WIN = 7168
decay_rate = 0.8
learn_rate = 0.05
small_term = 1e-06

N = 4
NZ = 8
TOK = 512
ROWS = 224
COLS = 512
HALF = FF_WIN // 2
CHUNK = HALF // N
H = 128
MSG = ROWS + 16
POWER = 9.0
TOP = 15000.0
OFFS = (2, 1, 3, 0)
MESH = pl.DeviceIdType.MESH


def pick(i, values):
    out = values[-1]
    for n in range(len(values) - 2, -1, -1):
        out = jnp.where(i == n, values[n], out)
    return out


def encode(ref, value):
    groups = value.reshape(ROWS // 16, 16, H)
    peak = jnp.maximum(jnp.max(jnp.abs(groups), axis=0), 1e-30).astype(jnp.bfloat16)
    scale = TOP / peak.astype(jnp.float32)
    u = groups * scale[None]
    u2 = u * u
    u4 = u2 * u2
    u8 = u4 * u4
    ref[pl.ds(0, ROWS), :] = (u8 * u).astype(jnp.bfloat16).reshape(ROWS, H)
    ref[pl.ds(ROWS, 16), :] = peak


def decode(ref):
    code = ref[pl.ds(0, ROWS), :].astype(jnp.float32).reshape(ROWS // 16, 16, H)
    scale = ref[pl.ds(ROWS, 16), :].astype(jnp.float32) * (1.0 / TOP)
    size = jnp.exp(jnp.log(jnp.maximum(jnp.abs(code), 1.2e-38)) * (1.0 / POWER))
    return (size * jnp.where(code < 0.0, -scale[None], scale[None])).reshape(ROWS, H)


def kernel(
    hid, gout, master, rprev, cprev,
    nw, upd_out, nrows_out, ncols_out,
    h_own, h_par, g_own, g_par, part, s1buf, r1buf, s2buf, r2buf, grad, mas, rp, cp,
    rowx, tall, colx, coly, colc, sizx, upd, nrow, ncol,
    ld_sem, xs_sem, xr_sem, s1s, r1s, s2s, r2s, zs, zr, cs, cr, ss, sr, a1s, a1r, a2s, a2r, out_sem,
):
    c = lax.axis_index("dp")
    s = lax.axis_index("seq")
    z = lax.axis_index("tensor")
    x = s // N
    y = s % N

    def wrap(v):
        return lax.rem(v + N, N)

    def at(px, py):
        return (c, wrap(px) * N + wrap(py), z)

    partner = (1 - c, s, z)
    peers_x = [at(x + d, y) for d in range(1, N)]
    peers_y = [at(x, y + d) for d in range(1, N)]
    peers_z = [(c, s, lax.rem(z + d, NZ)) for d in range(1, NZ)]

    barrier = pltpu.get_barrier_semaphore()
    everyone = [partner] + peers_x + peers_y + peers_z
    for peer in everyone:
        pl.semaphore_signal(barrier, inc=1, device_id=peer, device_id_type=MESH)

    def load(src, dst, n):
        copy = pltpu.make_async_copy(src, dst, ld_sem.at[n])
        return copy

    def columns(core, j):
        xi = wrap(x + pick(j, OFFS))
        return pl.ds(pl.multiple_of(core * HALF + xi * CHUNK, 128), CHUNK)

    loads = [load(gout, g_own, 4)]
    loads += [load(hid.at[:, columns(c, j)], h_own.at[j], j) for j in range(N)]
    loads += [load(master, mas, 5), load(rprev, rp, 6), load(cprev, cp, 7)]
    for copy in loads:
        copy.start()
    pl.semaphore_wait(barrier, len(everyone))

    def remote(src, dst, send, recv, peer):
        return pltpu.make_async_remote_copy(
            src_ref=src, dst_ref=dst, send_sem=send, recv_sem=recv, device_id=peer, device_id_type=MESH
        )

    swap_g = remote(gout, g_par, xs_sem.at[4], xr_sem.at[4], partner)
    swap_g.start()

    def swap_h(j):
        return remote(hid.at[:, columns(1 - c, j)], h_par.at[j], xs_sem.at[j], xr_sem.at[j], partner)

    for j in range(N):
        swap_h(j).start()

    right_x, left_x = at(x + 1, y), at(x - 1, y)
    right_y, left_y = at(x, y + 1), at(x, y - 1)
    link1 = [right_x, left_x, right_y, left_y]
    link2 = [right_y, left_y, right_x, left_x]

    def msg1(k, kind, i):
        return remote(s1buf.at[k, kind, i], r1buf.at[k, kind, i], s1s.at[k, kind, i], r1s.at[k, kind, i], link1[k])

    def msg2(k, kind):
        return remote(s2buf.at[k, kind], r2buf.at[k, kind], s2s.at[k, kind], r2s.at[k, kind], link2[k])

    def own(k):
        return pl.ds(k * H, H)

    def other(k):
        return pl.ds((k ^ 1) * H, H)

    def y_of(i):
        return wrap(y + pick(i, OFFS))

    loads[0].wait()
    swap_g.wait_recv()

    def send1(k, kind, i, value):
        encode(s1buf.at[k, kind, i], value)
        msg1(k, kind, i).start()

    def chunk(j, carry):
        load(hid.at[:, columns(c, j)], h_own.at[j], j).wait()
        dims = (((0,), (0,)), ((), ()))
        first = lax.dot_general(h_own[j], g_own[...], dims, preferred_element_type=jnp.float32)
        part[j] = first.reshape(N, ROWS, COLS)
        swap_h(j).wait_recv()
        second = lax.dot_general(h_par[j], g_par[...], dims, preferred_element_type=jnp.float32)
        part[j] += second.reshape(N, ROWS, COLS)

        @pl.when(j == 0)
        def _():
            def body(i, carry):
                for k in (0, 1):
                    send1(k, 0, i, part[0, y_of(i), :, own(k)])
                return carry

            lax.fori_loop(0, N, body, 0)

        for k in (2, 3):
            send1(k, 0, j, part[j, wrap(y + 2), :, own(k)])
        for k in (2, 3):
            send1(k, 1, j, part[j, wrap(y + (1 if k == 2 else -1)), :, other(k)])

        @pl.when(j == 1)
        def _():
            def body(i, carry):
                send1(0, 1, i, part[1, y_of(i), :, other(0)])
                return carry

            lax.fori_loop(0, N, body, 0)

        @pl.when(j == 2)
        def _():
            def body(i, carry):
                send1(1, 1, i, part[2, y_of(i), :, other(1)])
                return carry

            lax.fori_loop(0, N, body, 0)

        return carry

    lax.fori_loop(0, N, chunk, 0)

    def target(k, i):
        if k < 2:
            return part.at[1 + k, y_of(i), :, own(k)]
        return part.at[i, wrap(y + (1 if k == 2 else -1)), :, own(k)]

    def combine(i, carry):
        for k in range(4):
            msg1(k, 0, i).wait_recv()
            send1(k, 2, i, target(k, i)[...] + decode(r1buf.at[k, 0, i]))
        return carry

    lax.fori_loop(0, N, combine, 0)

    def mine(k, i):
        if k < 2:
            return part.at[3, y_of(i), :, own(k)]
        return part.at[i, y, :, own(k)]

    def send2(k, kind, value):
        encode(s2buf.at[k, kind], value)
        msg2(k, kind).start()

    def settle(i, carry):
        for k in range(4):
            msg1(k, 1, i).wait_recv()
            msg1(k, 2, i).wait_recv()
        for k in range(4):
            mine(k, i)[...] += decode(r1buf.at[k, 2, i]) + decode(r1buf.at[k ^ 1, 1, i])

        @pl.when(i == 0)
        def _():
            for k in range(4):
                send2(k, 0, mine(k, 0)[...])

        for step in (0, 1):

            @pl.when(i == 1 + step)
            def _():
                for k in (step, 2 + step):
                    send2(k, 1, mine(k ^ 1, 1 + step)[...])

        return carry

    lax.fori_loop(0, N - 1, settle, 0)
    for k in range(4):
        msg2(k, 0).wait_recv()
        send2(k, 2, mine(k, 1 + (k & 1))[...] + decode(r2buf.at[k, 0]))
    settle(jnp.int32(3), 0)
    for k in range(4):
        msg2(k, 1).wait_recv()
    for k in range(4):
        msg2(k, 2).wait_recv()
    for k in range(4):
        grad[:, own(k)] = mine(k, 3)[...] + decode(r2buf.at[k, 2]) + decode(r2buf.at[k ^ 1, 1])

    g = grad[...]
    squares = g * g + small_term
    folded = squares[:, 0:128] + squares[:, 128:256] + squares[:, 256:384] + squares[:, 384:512]
    tall[pl.ds(0, ROWS), :] = folded
    tall[pl.ds(ROWS, 256 - ROWS), :] = jnp.zeros((256 - ROWS, 128), jnp.float32)
    rowx[z] = jnp.sum(tall[...].T.reshape(16, 8, 256), axis=0)

    def exchange(ref, slot, peers, send, recv):
        copies = [remote(ref.at[slot], ref.at[slot], send.at[n], recv.at[n], peer) for n, peer in enumerate(peers)]
        for copy in copies:
            copy.start()
        for copy in copies:
            copy.wait_recv()
        return copies

    pending = exchange(rowx, z, peers_z, zs, zr)
    loads[6].wait()
    loads[7].wait()
    row_total = jnp.sum(jnp.sum(rowx[...], axis=0), axis=0, keepdims=True)
    new_rows = decay_rate * rp[...] + (1.0 - decay_rate) * row_total[:, 0:ROWS] / D
    nrow[...] = new_rows
    wide = jnp.concatenate([new_rows, jnp.ones((1, 256 - ROWS), jnp.float32)], axis=1)
    row_scale = lax.rsqrt(jnp.broadcast_to(wide, (128, 256)).T[0:ROWS, :])
    scaled = g * jnp.concatenate([row_scale] * 4, axis=1)

    col_sum = jnp.sum(squares, axis=0, keepdims=True)
    col_raw = jnp.sum(scaled * scaled, axis=0, keepdims=True)
    line = lax.broadcasted_iota(jnp.int32, (8, COLS), 0)
    colx[x] = jnp.where(line == 0, col_sum, jnp.where(line == 1, col_raw, 0.0))
    pending += exchange(colx, x, peers_x, cs.at[0], cr.at[0])
    coly[y] = colx[0] + colx[1] + colx[2] + colx[3]
    pending += exchange(coly, y, peers_y, cs.at[1], cr.at[1])
    colc[c] = coly[0] + coly[1] + coly[2] + coly[3]
    pending += exchange(colc, c, [partner], cs.at[2], cr.at[2])
    both = colc[0] + colc[1]
    new_cols = decay_rate * cp[...] + (1.0 - decay_rate) * both[0:1] / FF_WIN
    ncol[...] = new_cols
    ratio = both[1:2] / new_cols
    short = ratio[:, 0:128] + ratio[:, 128:256] + ratio[:, 256:384] + ratio[:, 384:512]
    sizx[z] = jnp.where(lax.broadcasted_iota(jnp.int32, (8, 128), 0) == 0, short, 0.0)
    pending += exchange(sizx, z, peers_z, ss, sr)
    raw_total = jnp.sum(jnp.sum(jnp.sum(sizx[...], axis=0), axis=0, keepdims=True), axis=1, keepdims=True)
    size = jnp.sqrt(raw_total / (FF_WIN * D))
    clip = 1.0 / jnp.maximum(1.0, size)
    update = scaled * (lax.rsqrt(new_cols) * clip)
    loads[5].wait()
    nw[s] = (mas[...] - learn_rate * update).astype(jnp.bfloat16)

    def block(px, py):
        return wrap(px) * N + wrap(py)

    def spread(k):
        return pl.ds((k // 2) * 2 * H, 2 * H)

    def ag(sems, index, src, cols, peer):
        send, recv = sems
        return remote(nw.at[src, :, cols], nw.at[src, :, cols], send.at[index], recv.at[index], peer)

    def source(k, n):
        step = (0, -1, 1, 2)[n]
        return block(x + step, y) if k < 2 else block(x, y + step)

    def first(k):
        return ag((a1s, a1r), (k, 0), s, spread(k), link1[k])

    def first_in(k):
        return ag((a1s, a1r), (k, 0), source(k, 1 + (k & 1)), spread(k), link1[k])

    def relay(k):
        return ag((a1s, a1r), (k, 1), source(k, 1 + (k & 1)), own(k), link1[k])

    def second(k, n):
        return ag((a2s, a2r), (k, n, 0), source(k, n), spread(k), link2[k])

    def beside(k, n):
        step = (0, -1, 1, 2)[n]
        back = -1 if (k & 1) == 0 else 1
        return block(x + step, y + back) if k < 2 else block(x + back, y + step)

    def third(k, n):
        return ag((a2s, a2r), (k, n, 1), beside(k, n), own(k), link2[k])

    sends = []

    def go(copy):
        copy.start()
        sends.append(copy)

    for k in range(4):
        go(first(k))
    for k in range(4):
        go(second(k, 0))
    upd[...] = update
    for k in (0, 2, 1, 3):
        first_in(k).wait_recv()
        go(relay(k))
        pair = k & 2
        go(second(pair, 1 + (k & 1)))
        go(second(pair + 1, 1 + (k & 1)))
    saves = [
        pltpu.make_async_copy(upd, upd_out, out_sem.at[0]),
        pltpu.make_async_copy(nrow, nrows_out, out_sem.at[1]),
        pltpu.make_async_copy(ncol, ncols_out, out_sem.at[2]),
    ]
    for copy in saves:
        copy.start()
    for k in range(4):
        second(k, 0).wait_recv()
        go(third(k, 0))
    for pair in (0, 2):
        for k in (pair, pair + 1):
            relay(k).wait_recv()
        for k in (pair, pair + 1):
            go(second(k, 3))
    for n in (1, 2, 3):
        for k in range(4):
            second(k, n).wait_recv()
            go(third(k, n))
    for n in range(4):
        for k in range(4):
            third(k, n).wait_recv()

    for copy in sends + pending:
        copy.wait_send()
    swap_g.wait_send()
    for j in range(N):
        swap_h(j).wait_send()

    def drain(i, carry):
        for k in range(4):
            for kind in range(3):
                msg1(k, kind, i).wait_send()
        return carry

    lax.fori_loop(0, N, drain, 0)
    for k in range(4):
        for kind in range(3):
            msg2(k, kind).wait_send()
    for copy in saves:
        copy.wait()


def per_device(hidden, grad_out, master_weight, row_prev, col_prev):
    any_space = pl.BlockSpec(memory_space=pl.ANY)
    f32, bf16 = jnp.float32, jnp.bfloat16
    dma = pltpu.SemaphoreType.DMA
    nw, upd, nrows, ncols = pl.pallas_call(
        kernel,
        out_shape=(
            jax.ShapeDtypeStruct((N * N, ROWS, COLS), bf16),
            jax.ShapeDtypeStruct((ROWS, COLS), f32),
            jax.ShapeDtypeStruct((1, ROWS), f32),
            jax.ShapeDtypeStruct((1, COLS), f32),
        ),
        in_specs=[any_space] * 5,
        out_specs=(pl.BlockSpec(memory_space=pltpu.VMEM), any_space, any_space, any_space),
        scratch_shapes=[
            pltpu.VMEM((N, TOK, CHUNK), bf16),
            pltpu.VMEM((N, TOK, CHUNK), bf16),
            pltpu.VMEM((TOK, COLS), bf16),
            pltpu.VMEM((TOK, COLS), bf16),
            pltpu.VMEM((N, N, ROWS, COLS), f32),
            pltpu.VMEM((4, 3, N, MSG, H), bf16),
            pltpu.VMEM((4, 3, N, MSG, H), bf16),
            pltpu.VMEM((4, 3, MSG, H), bf16),
            pltpu.VMEM((4, 3, MSG, H), bf16),
            pltpu.VMEM((ROWS, COLS), f32),
            pltpu.VMEM((ROWS, COLS), f32),
            pltpu.VMEM((1, ROWS), f32),
            pltpu.VMEM((1, COLS), f32),
            pltpu.VMEM((NZ, 8, 256), f32),
            pltpu.VMEM((256, 128), f32),
            pltpu.VMEM((N, 8, COLS), f32),
            pltpu.VMEM((N, 8, COLS), f32),
            pltpu.VMEM((2, 8, COLS), f32),
            pltpu.VMEM((NZ, 8, 128), f32),
            pltpu.VMEM((ROWS, COLS), f32),
            pltpu.VMEM((1, ROWS), f32),
            pltpu.VMEM((1, COLS), f32),
            dma((8,)), dma((5,)), dma((5,)),
            dma((4, 3, N)), dma((4, 3, N)), dma((4, 3)), dma((4, 3)),
            dma((NZ - 1,)), dma((NZ - 1,)), dma((3, 3)), dma((3, 3)), dma((NZ - 1,)), dma((NZ - 1,)),
            dma((4, 2)), dma((4, 2)), dma((4, 4, 2)), dma((4, 4, 2)), dma((3,)),
        ],
        compiler_params=pltpu.CompilerParams(
            collective_id=0, has_side_effects=True, vmem_limit_bytes=60 * 1024 * 1024
        ),
    )(hidden, grad_out, master_weight, row_prev.reshape(1, ROWS), col_prev.reshape(1, COLS))
    return nw.reshape(HALF, COLS), upd, nrows.reshape(ROWS), ncols.reshape(COLS)


def solution(mesh):
    return jax.shard_map(
        per_device,
        mesh=mesh,
        in_specs=(
            P(("dp", "seq"), None),
            P(("dp", "seq"), "tensor"),
            P(("dp", "seq"), "tensor"),
            P(("dp", "seq")),
            P("tensor"),
        ),
        out_specs=(P("dp", "tensor"), P(("dp", "seq"), "tensor"), P(("dp", "seq")), P("tensor")),
        check_vma=False,
    )
```

time: 363 us -> 89.2 us (0.25)
  waiting for transfers between devices: 172 us -> 0 us
  blocking collectives: 154 us -> 0 us
  Pallas kernels: 0 us -> 81.7 us
  between operations: 14.8 us -> 0.67 us
  matrix products: 10.5 us -> 0 us
  other arithmetic: 5.03 us -> 0 us
    psum x3 -> x0, blocking collectives: 154 us -> none  [the longest x1 74.1 us: per_device(): raw_total = lax.psum(jnp.sum(raw * raw), ('dp', 'seq', 'tensor'))]
    reduce_scatter x1 -> x0, waiting for transfers between devices: 120 us -> none  [per_device(): lax.psum_scatter(lax.dot_general(hidden, grad_out, (((0,), (0,)), ((), ()...]
    pallas_call x0 -> x1, Pallas kernels: none -> 81.7 us  [per_device(): pl.pallas_call(kernel, out_shape=(jax.ShapeDtypeStruct((N * N, ROWS, COLS...]
    all_gather x1 -> x0, waiting for transfers between devices: 51.3 us -> none  [per_device(): new_weight = lax.all_gather(fresh, 'seq', axis=0, tiled=True)]
    dot_general x1 -> x0, matrix products: 10.5 us -> none  [per_device(): lax.dot_general(hidden, grad_out, (((0,), (0,)), ((), ())), preferred_ele...]
  transfers between devices with their start and end apart: 2 -> 0, of which waited for: 2 -> 0; matrix products, arithmetic and copies ran while one was open for 0% -> 0% of each run, Pallas kernels for 0% -> 0%
where the time goes in v1:
time: 89.2 us; the launch traced here: 88.4 us
  Pallas kernels  81.7 us (92%)
  local copies, waits for them, and re-layouts  6.08 us (7%)
    pallas_call x1, Pallas kernels, per_device(): pl.pallas_call(kernel, out_shape=(jax.ShapeDtypeStruct((N * N, ROWS, COLS...  81.7 us
    unnamed x10, local copies, waits for them, and re-layouts  6.08 us

profile of v1, /device:TPU:2, one launch (start us, length us, event | category | flops | bytes accessed | tf_op | source)
XLA Modules:
  0.0 88.4 jit_solution(5817744153432141358)
XLA Ops:
  0.6 81.7 %shard_map.84 = (bf16[16,224,512]{2,1,0:T(8,128)(2,1)}, f32[224,512]{1,0:T(8,128)}, f32[1,224]{1,0:T(1,128)}, f32[1,512]{1,0:T(1,128)}) custom-call(bf16[512,7168]{1,0:T(8,128)(2,1)} %hid.1, bf16[512,512]{1,0:T(8,128)(2,1)} %gout.1, f32[224,512]{1,0:T(8,128)} %master.1, f32[1,224]{1,0:T(1,128)} %bitcast.8, f32[1,512]{1,0:T(1,128)} %bitcast.6), custom_call_target="tpu_custom_call" | custom-call | tf_op jit(solution)/shard_map/pallas_call | solution.py:384
  82.3 0.0 copy-start
  82.3 0.0 copy-start.2
  82.4 0.0 copy-start.1
  82.4 4.2 %copy.13 = bf16[3584,512]{1,0:T(8,128)(2,1)} copy(bf16[3584,512]{1,0:T(8,128)(2,1)} %bitcast.5) | data formatting | bytes 7340032
  86.5 0.0 copy-done
  86.5 0.8 copy.14
  87.3 0.0 copy-done.2
  87.3 0.6 copy.15
  87.9 0.0 copy-done.1
  87.9 0.6 copy.16
Async XLA Ops:
  82.3 4.2 %copy-start = (f32[224,512]{1,0:T(8,128)S(1)}, f32[224,512]{1,0:T(8,128)}, u32[]{:S(2)}) copy-start(f32[224,512]{1,0:T(8,128)} %get-tuple-element.17) | copy-start | bytes 1376260
  82.3 5.0 %copy-start.2 = (f32[1,224]{1,0:T(1,128)S(1)}, f32[1,224]{1,0:T(1,128)}, u32[]{:S(2)}) copy-start(f32[1,224]{1,0:T(1,128)} %get-tuple-element.10) | copy-start | bytes 2692
  82.4 5.5 %copy-start.1 = (f32[1,512]{1,0:T(1,128)S(1)}, f32[1,512]{1,0:T(1,128)}, u32[]{:S(2)}) copy-start(f32[1,512]{1,0:T(1,128)} %get-tuple-element.11) | copy-start | bytes 6148

commit v2 on v1

v2 whole, which is shorter than its diff:
```python
import jax
import jax.numpy as jnp
from jax import lax
from jax.experimental import pallas as pl
from jax.experimental.pallas import tpu as pltpu
from jax.sharding import PartitionSpec as P

D = 4096
FF_WIN = 7168
decay_rate = 0.8
learn_rate = 0.05
small_term = 1e-06

N = 4
NZ = 8
TOK = 512
ROWS = 224
COLS = 512
HALF = FF_WIN // 2
CHUNK = HALF // N
H = 128
MSG = ROWS + 16
POWER = 9.0
TOP = 15000.0
OFFS = (2, 1, 3, 0)
MESH = pl.DeviceIdType.MESH


def pick(i, values):
    out = values[-1]
    for n in range(len(values) - 2, -1, -1):
        out = jnp.where(i == n, values[n], out)
    return out


def encode(ref, value):
    groups = value.reshape(ROWS // 16, 16, H)
    peak = jnp.maximum(jnp.max(jnp.abs(groups), axis=0), 1e-30).astype(jnp.bfloat16)
    scale = TOP / peak.astype(jnp.float32)
    u = groups * scale[None]
    u2 = u * u
    u4 = u2 * u2
    u8 = u4 * u4
    ref[pl.ds(0, ROWS), :] = (u8 * u).astype(jnp.bfloat16).reshape(ROWS, H)
    ref[pl.ds(ROWS, 16), :] = peak


def decode(ref):
    code = ref[pl.ds(0, ROWS), :].astype(jnp.float32).reshape(ROWS // 16, 16, H)
    scale = ref[pl.ds(ROWS, 16), :].astype(jnp.float32) * (1.0 / TOP)
    size = jnp.exp(jnp.log(jnp.maximum(jnp.abs(code), 1.2e-38)) * (1.0 / POWER))
    return (size * jnp.where(code < 0.0, -scale[None], scale[None])).reshape(ROWS, H)


def kernel(
    hid, gout, master, rprev, cprev,
    nw, upd, nrow, ncol,
    h_own, h_par, g_own, g_par, flat, s1buf, r1buf, s2buf, r2buf, grad, mas, rp, cp,
    rowx, tall, plane, colc, sizx,
    ld_sem, xs_sem, xr_sem, s1s, r1s, s2s, r2s, zs, zr, cs, cr, ps, pr, ss, sr, ws, wr, bs, br, a2s, a2r, chain,
):
    c = lax.axis_index("dp")
    s = lax.axis_index("seq")
    z = lax.axis_index("tensor")
    x = s // N
    y = s % N

    def wrap(v):
        return lax.rem(v + N, N)

    def at(px, py):
        return (c, wrap(px) * N + wrap(py), z)

    partner = (1 - c, s, z)
    peers_plane = [at(x + d // N, y + d % N) for d in range(1, N * N)]
    peers_z = [(c, s, lax.rem(z + d, NZ)) for d in range(1, NZ)]
    right_x, left_x = at(x + 1, y), at(x - 1, y)
    right_y, left_y = at(x, y + 1), at(x, y - 1)
    link1 = [right_x, left_x, right_y, left_y]
    link2 = [right_y, left_y, right_x, left_x]
    near = link1 + [peers_z[0], peers_z[-1]]

    barrier = pltpu.get_barrier_semaphore()
    for peer in [partner] + near:
        pl.semaphore_signal(barrier, inc=1, device_id=peer, device_id_type=MESH)

    first = 1 - y // 2
    near_window = pl.ds(pl.multiple_of(first * 384, 128), 512)
    far_window = pl.ds(pl.multiple_of((1 - first) * 512, 128), 384)

    def start_of(core, j):
        return core * HALF + wrap(x + pick(j, OFFS)) * CHUNK

    def columns(core, j):
        return pl.ds(pl.multiple_of(start_of(core, j), 128), CHUNK)

    def load(src, dst, n):
        return pltpu.make_async_copy(src, dst, ld_sem.at[n])

    def load_h(j):
        return load(hid.at[:, columns(c, j)], h_own.at[j], j)

    load_g = load(gout, g_own, 4)
    small = [load(master, mas, 5), load(rprev, rp, 6), load(cprev, cp, 7)]
    load_g.start()
    for j in range(N):
        load_h(j).start()
    pl.semaphore_wait(barrier, 1 + len(near))

    def remote(src, dst, send, recv, peer):
        return pltpu.make_async_remote_copy(
            src_ref=src, dst_ref=dst, send_sem=send, recv_sem=recv, device_id=peer, device_id_type=MESH
        )

    def tell(n):
        for peer in near:
            pl.semaphore_signal(chain.at[n], inc=1, device_id=peer, device_id_type=MESH)

    def told(n):
        pl.semaphore_wait(chain.at[n], len(near))

    left_half, right_half = pl.ds(0, 2 * H), pl.ds(2 * H, 2 * H)
    base = start_of(1 - c, 0)
    src_near = pl.ds(pl.multiple_of(base + first * 384, 128), 512)
    src_far = pl.ds(pl.multiple_of(base + (1 - first) * 512, 128), 384)

    def swap(n, src, dst):
        return remote(src, dst, xs_sem.at[n], xr_sem.at[n], partner)

    def swap_h(j):
        return swap(j, hid.at[:, columns(1 - c, j)], h_par.at[j])

    swap_near = swap(0, hid.at[:, src_near], h_par.at[0, :, near_window])
    swap_far = swap(6, hid.at[:, src_far], h_par.at[0, :, far_window])
    swap_ga = swap(4, gout.at[:, left_half], g_par.at[:, left_half])
    swap_gb = swap(5, gout.at[:, right_half], g_par.at[:, right_half])
    swaps = [swap_ga, swap_near, swap_far, swap_gb] + [swap_h(j) for j in range(1, N)]
    for copy in swaps:
        copy.start()
    for copy in small:
        copy.start()
    tell(0)

    def msg1(k, kind, i):
        return remote(s1buf.at[k, kind, i], r1buf.at[k, kind, i], s1s.at[k, kind, i], r1s.at[k, kind, i], link1[k])

    def msg2(k, kind):
        return remote(s2buf.at[k, kind], r2buf.at[k, kind], s2s.at[k, kind], r2s.at[k, kind], link2[k])

    def own(k):
        return pl.ds(k * H, H)

    def other(k):
        return pl.ds((k ^ 1) * H, H)

    def y_of(i):
        return pick(i, (wrap(y + 2), wrap(y + 2) + 1 - 2 * (y % 2), y + 1 - 2 * (y % 2), y))

    def part(j, v, cols):
        return flat.at[j, pl.ds(pl.multiple_of(v * ROWS, 32), ROWS), cols]

    def send1(k, kind, i, value):
        encode(s1buf.at[k, kind, i], value)
        msg1(k, kind, i).start()

    dims = (((0,), (0,)), ((), ()))

    def dot(h, g):
        return lax.dot_general(h, g, dims, preferred_element_type=jnp.float32)

    def ahead(k):
        return 1 if (k & 1) == 0 else -1

    def send_b(j):
        for k in (2, 3):
            send1(k, 0, j, part(j, wrap(y + 2), own(k))[...])
        for k in (2, 3):
            send1(k, 1, j, part(j, wrap(y + ahead(k)), other(k))[...])

    def send_a(i, carry):
        for k in (0, 1):
            send1(k, 0, i, part(0, y_of(i), own(k))[...])
        return carry

    load_g.wait()
    load_h(0).wait()
    flat[0] = dot(h_own[0], g_own[...])
    swap_ga.wait_recv()
    swap_near.wait_recv()
    flat[0, near_window, left_half] += dot(h_par[0, :, near_window], g_par[:, left_half])
    lax.fori_loop(0, 2, send_a, 0)
    swap_far.wait_recv()
    flat[0, far_window, left_half] += dot(h_par[0, :, far_window], g_par[:, left_half])
    lax.fori_loop(2, N, send_a, 0)
    swap_gb.wait_recv()
    flat[0, :, right_half] += dot(h_par[0], g_par[:, right_half])
    send_b(0)
    told(0)
    tell(1)

    def chunk(j, carry):
        load_h(j).wait()
        flat[j] = dot(h_own[j], g_own[...])
        swap_h(j).wait_recv()
        flat[j] += dot(h_par[j], g_par[...])
        send_b(j)

        for k in (0, 1):

            @pl.when(j == 1 + k)
            def _():
                def body(i, carry):
                    send1(k, 1, i, part(1 + k, y_of(i), other(k))[...])
                    return carry

                lax.fori_loop(0, N, body, 0)

        return carry

    lax.fori_loop(1, N, chunk, 0)
    told(1)
    tell(2)

    def target(k, i):
        if k < 2:
            return part(1 + k, y_of(i), own(k))
        return part(i, wrap(y + ahead(k)), own(k))

    def combine(i, carry):
        for k in range(4):
            msg1(k, 0, i).wait_recv()
            send1(k, 2, i, target(k, i)[...] + decode(r1buf.at[k, 0, i]))
        return carry

    lax.fori_loop(0, N, combine, 0)

    def mine(k, i):
        if k < 2:
            return part(3, y_of(i), own(k))
        return part(i, y, own(k))

    def beyond(k, cols):
        if k < 2:
            return part(3, wrap(y + ahead(k)), cols)
        return part(1 + (k & 1), y, cols)

    def send2(k, kind, value):
        encode(s2buf.at[k, kind], value)
        msg2(k, kind).start()

    def settle(i, carry):
        for k in range(4):
            msg1(k, 1, i).wait_recv()
            msg1(k, 2, i).wait_recv()
        for k in range(4):
            mine(k, i)[...] += decode(r1buf.at[k, 2, i]) + decode(r1buf.at[k ^ 1, 1, i])

        @pl.when(i == 0)
        def _():
            for k in range(4):
                send2(k, 0, mine(k, 0)[...])

        @pl.when(i == 2)
        def _():
            for k in range(4):
                send2(k, 1, beyond(k, other(k))[...])

        return carry

    lax.fori_loop(0, N - 1, settle, 0)
    for k in range(4):
        msg2(k, 0).wait_recv()
        send2(k, 2, beyond(k, own(k))[...] + decode(r2buf.at[k, 0]))
    settle(jnp.int32(3), 0)
    told(2)
    for k in range(4):
        msg2(k, 1).wait_recv()
    for k in range(4):
        msg2(k, 2).wait_recv()
    for k in range(4):
        grad[:, own(k)] = mine(k, 3)[...] + decode(r2buf.at[k, 2]) + decode(r2buf.at[k ^ 1, 1])

    g = grad[...]
    squares = g * g + small_term
    folded = squares[:, 0:128] + squares[:, 128:256] + squares[:, 256:384] + squares[:, 384:512]
    tall[pl.ds(0, ROWS), :] = folded
    tall[pl.ds(ROWS, 256 - ROWS), :] = jnp.zeros((256 - ROWS, 128), jnp.float32)
    rowx[z] = jnp.sum(tall[...].T.reshape(16, 8, 256), axis=0)

    def exchange(ref, slot, peers, send, recv):
        copies = [remote(ref.at[slot], ref.at[slot], send.at[n], recv.at[n], peer) for n, peer in enumerate(peers)]
        for copy in copies:
            copy.start()
        return copies

    def arrive(copies):
        for copy in copies:
            copy.wait_recv()
        return copies

    pending = exchange(rowx, z, peers_z, zs, zr)
    col_sum = jnp.sum(squares, axis=0, keepdims=True)
    for copy in small:
        copy.wait()
    arrive(pending)
    row_total = jnp.sum(jnp.sum(rowx[...], axis=0), axis=0, keepdims=True)
    new_rows = decay_rate * rp[...] + (1.0 - decay_rate) * row_total[:, 0:ROWS] / D
    nrow[...] = new_rows
    wide = jnp.concatenate([new_rows, jnp.ones((1, 256 - ROWS), jnp.float32)], axis=1)
    row_scale = jnp.broadcast_to(lax.rsqrt(wide), (128, 256)).T[0:ROWS, :]
    scaled = g * jnp.concatenate([row_scale] * 4, axis=1)

    colc[c, pl.ds(0, 1), :] = col_sum
    colc[c, pl.ds(1, 1), :] = jnp.sum(scaled * scaled, axis=0, keepdims=True)
    pending += arrive(exchange(colc, c, [partner], cs, cr))
    plane[s] = colc[0] + colc[1]
    pending += arrive(exchange(plane, s, peers_plane, ps, pr))
    both = jnp.sum(plane[...], axis=0)
    new_cols = decay_rate * cp[...] + (1.0 - decay_rate) * both[0:1] / FF_WIN
    ncol[...] = new_cols
    ratio = both[1:2] / new_cols
    short = ratio[:, 0:128] + ratio[:, 128:256] + ratio[:, 256:384] + ratio[:, 384:512]
    sizx[z] = jnp.where(lax.broadcasted_iota(jnp.int32, (8, 128), 0) == 0, short, 0.0)
    last = exchange(sizx, z, peers_z, ss, sr)
    raw = scaled * lax.rsqrt(new_cols)
    pending += arrive(last)
    raw_total = jnp.sum(jnp.sum(jnp.sum(sizx[...], axis=0), axis=0, keepdims=True), axis=1, keepdims=True)
    size = jnp.sqrt(raw_total / (FF_WIN * D))
    update = raw * (1.0 / jnp.maximum(1.0, size))
    nw[s] = (mas[...] - learn_rate * update).astype(jnp.bfloat16)

    def block(px, py):
        return wrap(px) * N + wrap(py)

    def pair(k):
        return pl.ds((k // 2) * 2 * H, 2 * H)

    def gather(send, recv, src, cols, peer):
        return remote(nw.at[src, :, cols], nw.at[src, :, cols], send, recv, peer)

    from_link = [block(x - 1, y), block(x + 1, y), block(x, y - 1), block(x, y + 1)]
    opposite = [block(x + 2, y), block(x, y + 2)]

    def whole(k, src):
        return gather(ws.at[k], wr.at[k], src, pl.ds(0, COLS), link1[k])

    def relay(k, src):
        return gather(bs.at[k], br.at[k], src, pl.ds((k & 1) * 2 * H, 2 * H), link1[k])

    def second(k, n, src):
        return gather(a2s.at[k, n, 0], a2r.at[k, n, 0], src, pair(k), link2[k])

    def beside(k, n):
        step = (-1, 1, 2)[n]
        return block(x + step, y - ahead(k)) if k < 2 else block(x - ahead(k), y + step)

    def third(k, n):
        return gather(a2s.at[k, n, 1], a2r.at[k, n, 1], beside(k, n), own(k), link2[k])

    sends = []

    def go(copy):
        copy.start()
        sends.append(copy)

    for k in range(4):
        go(whole(k, s))
    upd[...] = update
    for k in (0, 2, 1, 3):
        whole(k, from_link[k]).wait_recv()
        go(relay(k, from_link[k]))
        for side in (0, 1):
            go(second((k & 2) + side, k & 1, from_link[k]))
    for k, axis in ((0, 0), (3, 1)):
        relay(k, opposite[axis]).wait_recv()
        for side in (0, 1):
            go(second(axis * 2 + side, 2, opposite[axis]))
    for n in range(3):
        for k in range(4):
            second(k, n, beside(k, n)).wait_recv()
            go(third(k, n))
    relay(1, opposite[0]).wait_recv()
    relay(2, opposite[1]).wait_recv()
    for n in range(3):
        for k in range(4):
            third(k, n).wait_recv()

    for copy in sends + pending + swaps:
        copy.wait_send()

    def drain(i, carry):
        for k in range(4):
            for kind in range(3):
                msg1(k, kind, i).wait_send()
        return carry

    lax.fori_loop(0, N, drain, 0)
    for k in range(4):
        for kind in range(3):
            msg2(k, kind).wait_send()


def writer(nw, upd, nrow, ncol, nw_out, upd_out, nrow_out, ncol_out, sem):
    quarter = N * N // 4
    pairs = [(nw.at[pl.ds(n * quarter, quarter)], nw_out.at[pl.ds(n * quarter, quarter)]) for n in range(4)]
    pairs += [(upd, upd_out), (nrow, nrow_out), (ncol, ncol_out)]
    copies = [pltpu.make_async_copy(src, dst, sem.at[n]) for n, (src, dst) in enumerate(pairs)]
    for copy in copies:
        copy.start()
    for copy in copies:
        copy.wait()


def per_device(hidden, grad_out, master_weight, row_prev, col_prev):
    hbm = pl.BlockSpec(memory_space=pltpu.HBM)
    vmem = pl.BlockSpec(memory_space=pltpu.VMEM)
    f32, bf16 = jnp.float32, jnp.bfloat16
    dma = pltpu.SemaphoreType.DMA
    results = (((N * N, ROWS, COLS), bf16), ((ROWS, COLS), f32), ((1, ROWS), f32), ((1, COLS), f32))
    held = pl.pallas_call(
        kernel,
        out_shape=tuple(pltpu.VMEM(shape, kind) for shape, kind in results),
        in_specs=[hbm] * 5,
        out_specs=(vmem,) * 4,
        scratch_shapes=[
            pltpu.VMEM((N, TOK, CHUNK), bf16),
            pltpu.VMEM((N, TOK, CHUNK), bf16),
            pltpu.VMEM((TOK, COLS), bf16),
            pltpu.VMEM((TOK, COLS), bf16),
            pltpu.VMEM((N, CHUNK, COLS), f32),
            pltpu.VMEM((4, 3, N, MSG, H), bf16),
            pltpu.VMEM((4, 3, N, MSG, H), bf16),
            pltpu.VMEM((4, 3, MSG, H), bf16),
            pltpu.VMEM((4, 3, MSG, H), bf16),
            pltpu.VMEM((ROWS, COLS), f32),
            pltpu.VMEM((ROWS, COLS), f32),
            pltpu.VMEM((1, ROWS), f32),
            pltpu.VMEM((1, COLS), f32),
            pltpu.VMEM((NZ, 8, 256), f32),
            pltpu.VMEM((256, 128), f32),
            pltpu.VMEM((N * N, 2, COLS), f32),
            pltpu.VMEM((2, 2, COLS), f32),
            pltpu.VMEM((NZ, 8, 128), f32),
            dma((8,)), dma((7,)), dma((7,)),
            dma((4, 3, N)), dma((4, 3, N)), dma((4, 3)), dma((4, 3)),
            dma((NZ - 1,)), dma((NZ - 1,)), dma((1,)), dma((1,)), dma((N * N - 1,)), dma((N * N - 1,)),
            dma((NZ - 1,)), dma((NZ - 1,)),
            dma((4,)), dma((4,)), dma((4,)), dma((4,)), dma((4, 3, 2)), dma((4, 3, 2)),
            pltpu.SemaphoreType.REGULAR((3,)),
        ],
        compiler_params=pltpu.CompilerParams(collective_id=0, has_side_effects=True, vmem_limit_bytes=62700000),
    )(hidden, grad_out, master_weight, row_prev.reshape(1, ROWS), col_prev.reshape(1, COLS))
    nw, upd, nrows, ncols = pl.pallas_call(
        writer,
        out_shape=tuple(jax.ShapeDtypeStruct(shape, kind) for shape, kind in results),
        in_specs=[vmem] * 4,
        out_specs=(hbm,) * 4,
        scratch_shapes=[dma((7,))],
        compiler_params=pltpu.CompilerParams(vmem_limit_bytes=1024 * 1024),
    )(*held)
    return nw.reshape(HALF, COLS), upd, nrows.reshape(ROWS), ncols.reshape(COLS)


def solution(mesh):
    return jax.shard_map(
        per_device,
        mesh=mesh,
        in_specs=(
            P(("dp", "seq"), None),
            P(("dp", "seq"), "tensor"),
            P(("dp", "seq"), "tensor"),
            P(("dp", "seq")),
            P("tensor"),
        ),
        out_specs=(P("dp", "tensor"), P(("dp", "seq"), "tensor"), P(("dp", "seq")), P("tensor")),
        check_vma=False,
    )
```

time: 89.2 us -> 79.9 us (0.90)
  local copies, waits for them, and re-layouts: 6.08 us -> 0 us
  Pallas kernels: 81.7 us -> 79.1 us
    unnamed x10 -> x0, local copies, waits for them, and re-layouts: 6.08 us -> none
    pallas_call x1 -> x2, Pallas kernels: 81.7 us -> 79.1 us  [the longest x1 77 us: per_device(): pl.pallas_call(kernel, out_shape=tuple((pltpu.VMEM(shape, kind) for shape...]
where the time goes in v2:
time: 79.9 us; the launch traced here: 79.7 us
  Pallas kernels  79.1 us (99%)
    pallas_call x1, Pallas kernels, per_device(): pl.pallas_call(kernel, out_shape=tuple((pltpu.VMEM(shape, kind) for shape...  77 us
    pallas_call x1, Pallas kernels, per_device(): pl.pallas_call(writer, out_shape=tuple((jax.ShapeDtypeStruct(shape, kind)...  2.04 us

profile of v2, /device:TPU:2, one launch (start us, length us, event | category | flops | bytes accessed | tf_op | source)
XLA Modules:
  0.0 79.7 jit_solution(14923292708724878677)
XLA Ops:
  0.6 77.0 %shard_map.84 = (bf16[16,224,512]{2,1,0:T(8,128)(2,1)S(1)}, f32[224,512]{1,0:T(8,128)S(1)}, f32[1,224]{1,0:T(1,128)S(1)}, f32[1,512]{1,0:T(1,128)S(1)}) custom-call(bf16[512,7168]{1,0:T(8,128)(2,1)} %hid.1, bf16[512,512]{1,0:T(8,128)(2,1)} %gout.1, f32[224,512]{1,0:T(8,128)} %master.1, f32[1,224]{1,0:T(1,128)} %bitcast.6, f32[1,512]{1,0:T(1,128)} %bitcast.5), custom_call_target="tpu_custom_call" | custom-call | tf_op jit(solution)/shard_map/pallas_call | solution.py:420
  77.7 2.0 %shard_map.85 = (bf16[16,224,512]{2,1,0:T(8,128)(2,1)}, f32[224,512]{1,0:T(8,128)}, f32[1,224]{1,0:T(1,128)}, f32[1,512]{1,0:T(1,128)}) custom-call(bf16[16,224,512]{2,1,0:T(8,128)(2,1)S(1)} %get-tuple-element.12.nw, f32[224,512]{1,0:T(8,128)S(1)} %get-tuple-element.13.upd, f32[1,224]{1,0:T(1,128)S(1)} %get-tuple-element.14.nrow, ...), custom_call_target="tpu_custom_call" | custom-call | tf_op jit(solution)/shard_map/pallas_call | solution.py:453

commit v3 on v2

--- a/solution.py
+++ b/solution.py
@@ -19,7 +19,8 @@
 HALF = FF_WIN // 2
 CHUNK = HALF // N
 H = 128
-MSG = ROWS + 16
+G = 8
+MSG = ROWS + G
 POWER = 9.0
 TOP = 15000.0
 OFFS = (2, 1, 3, 0)
@@ -34,7 +35,7 @@
 
 
 def encode(ref, value):
-    groups = value.reshape(ROWS // 16, 16, H)
+    groups = value.reshape(ROWS // G, G, H)
     peak = jnp.maximum(jnp.max(jnp.abs(groups), axis=0), 1e-30).astype(jnp.bfloat16)
     scale = TOP / peak.astype(jnp.float32)
     u = groups * scale[None]
@@ -42,12 +43,12 @@
     u4 = u2 * u2
     u8 = u4 * u4
     ref[pl.ds(0, ROWS), :] = (u8 * u).astype(jnp.bfloat16).reshape(ROWS, H)
-    ref[pl.ds(ROWS, 16), :] = peak
+    ref[pl.ds(ROWS, G), :] = peak
 
 
 def decode(ref):
-    code = ref[pl.ds(0, ROWS), :].astype(jnp.float32).reshape(ROWS // 16, 16, H)
-    scale = ref[pl.ds(ROWS, 16), :].astype(jnp.float32) * (1.0 / TOP)
+    code = ref[pl.ds(0, ROWS), :].astype(jnp.float32).reshape(ROWS // G, G, H)
+    scale = ref[pl.ds(ROWS, G), :].astype(jnp.float32) * (1.0 / TOP)
     size = jnp.exp(jnp.log(jnp.maximum(jnp.abs(code), 1.2e-38)) * (1.0 / POWER))
     return (size * jnp.where(code < 0.0, -scale[None], scale[None])).reshape(ROWS, H)
 
@@ -119,7 +120,6 @@
     def told(n):
         pl.semaphore_wait(chain.at[n], len(near))
 
-    left_half, right_half = pl.ds(0, 2 * H), pl.ds(2 * H, 2 * H)
     base = start_of(1 - c, 0)
     src_near = pl.ds(pl.multiple_of(base + first * 384, 128), 512)
     src_far = pl.ds(pl.multiple_of(base + (1 - first) * 512, 128), 384)
@@ -132,9 +132,8 @@
 
     swap_near = swap(0, hid.at[:, src_near], h_par.at[0, :, near_window])
     swap_far = swap(6, hid.at[:, src_far], h_par.at[0, :, far_window])
-    swap_ga = swap(4, gout.at[:, left_half], g_par.at[:, left_half])
-    swap_gb = swap(5, gout.at[:, right_half], g_par.at[:, right_half])
-    swaps = [swap_ga, swap_near, swap_far, swap_gb] + [swap_h(j) for j in range(1, N)]
+    swap_g = swap(4, gout, g_par)
+    swaps = [swap_g, swap_near, swap_far] + [swap_h(j) for j in range(1, N)]
     for copy in swaps:
         copy.start()
     for copy in small:
@@ -171,9 +170,11 @@
     def ahead(k):
         return 1 if (k & 1) == 0 else -1
 
-    def send_b(j):
+    def send_b1(j):
         for k in (2, 3):
             send1(k, 0, j, part(j, wrap(y + 2), own(k))[...])
+
+    def send_b2(j):
         for k in (2, 3):
             send1(k, 1, j, part(j, wrap(y + ahead(k)), other(k))[...])
 
@@ -185,16 +186,16 @@
     load_g.wait()
     load_h(0).wait()
     flat[0] = dot(h_own[0], g_own[...])
-    swap_ga.wait_recv()
+    swap_g.wait_recv()
     swap_near.wait_recv()
-    flat[0, near_window, left_half] += dot(h_par[0, :, near_window], g_par[:, left_half])
-    lax.fori_loop(0, 2, send_a, 0)
+    flat[0, near_window, :] += dot(h_par[0, :, near_window], g_par[...])
+    send_a(0, 0)
+    send_b1(0)
+    send_a(1, 0)
     swap_far.wait_recv()
-    flat[0, far_window, left_half] += dot(h_par[0, :, far_window], g_par[:, left_half])
+    flat[0, far_window, :] += dot(h_par[0, :, far_window], g_par[...])
     lax.fori_loop(2, N, send_a, 0)
-    swap_gb.wait_recv()
-    flat[0, :, right_half] += dot(h_par[0], g_par[:, right_half])
-    send_b(0)
+    send_b2(0)
     told(0)
     tell(1)
 
@@ -203,7 +204,8 @@
         flat[j] = dot(h_own[j], g_own[...])
         swap_h(j).wait_recv()
         flat[j] += dot(h_par[j], g_par[...])
-        send_b(j)
+        send_b1(j)
+        send_b2(j)
 
         for k in (0, 1):
 
@@ -285,7 +287,7 @@
     folded = squares[:, 0:128] + squares[:, 128:256] + squares[:, 256:384] + squares[:, 384:512]
     tall[pl.ds(0, ROWS), :] = folded
     tall[pl.ds(ROWS, 256 - ROWS), :] = jnp.zeros((256 - ROWS, 128), jnp.float32)
-    rowx[z] = jnp.sum(tall[...].T.reshape(16, 8, 256), axis=0)
+    rowx[z] = jnp.sum(tall[...].T, axis=0, keepdims=True)
 
     def exchange(ref, slot, peers, send, recv):
         copies = [remote(ref.at[slot], ref.at[slot], send.at[n], recv.at[n], peer) for n, peer in enumerate(peers)]
@@ -303,7 +305,7 @@
     for copy in small:
         copy.wait()
     arrive(pending)
-    row_total = jnp.sum(jnp.sum(rowx[...], axis=0), axis=0, keepdims=True)
+    row_total = jnp.sum(rowx[...], axis=0)
     new_rows = decay_rate * rp[...] + (1.0 - decay_rate) * row_total[:, 0:ROWS] / D
     nrow[...] = new_rows
     wide = jnp.concatenate([new_rows, jnp.ones((1, 256 - ROWS), jnp.float32)], axis=1)
@@ -320,11 +322,11 @@
     ncol[...] = new_cols
     ratio = both[1:2] / new_cols
     short = ratio[:, 0:128] + ratio[:, 128:256] + ratio[:, 256:384] + ratio[:, 384:512]
-    sizx[z] = jnp.where(lax.broadcasted_iota(jnp.int32, (8, 128), 0) == 0, short, 0.0)
+    sizx[z] = short
     last = exchange(sizx, z, peers_z, ss, sr)
     raw = scaled * lax.rsqrt(new_cols)
     pending += arrive(last)
-    raw_total = jnp.sum(jnp.sum(jnp.sum(sizx[...], axis=0), axis=0, keepdims=True), axis=1, keepdims=True)
+    raw_total = jnp.sum(jnp.sum(sizx[...], axis=0), axis=1, keepdims=True)
     size = jnp.sqrt(raw_total / (FF_WIN * D))
     update = raw * (1.0 / jnp.maximum(1.0, size))
     nw[s] = (mas[...] - learn_rate * update).astype(jnp.bfloat16)
@@ -341,8 +343,8 @@
     from_link = [block(x - 1, y), block(x + 1, y), block(x, y - 1), block(x, y + 1)]
     opposite = [block(x + 2, y), block(x, y + 2)]
 
-    def whole(k, src):
-        return gather(ws.at[k], wr.at[k], src, pl.ds(0, COLS), link1[k])
+    def direct(k, part_of, src):
+        return gather(ws.at[k, part_of], wr.at[k, part_of], src, pl.ds(part_of * 2 * H, 2 * H), link1[k])
 
     def relay(k, src):
         return gather(bs.at[k], br.at[k], src, pl.ds((k & 1) * 2 * H, 2 * H), link1[k])
@@ -364,13 +366,19 @@
         sends.append(copy)
 
     for k in range(4):
-        go(whole(k, s))
+        go(direct(k, k // 2, s))
+    for k in range(4):
+        go(direct(k, 1 - k // 2, s))
     upd[...] = update
-    for k in (0, 2, 1, 3):
-        whole(k, from_link[k]).wait_recv()
-        go(relay(k, from_link[k]))
+    for k in (0, 3, 1, 2):
+        direct(k, k // 2, from_link[k]).wait_recv()
+        if k in (0, 3):
+            go(relay(k, from_link[k]))
         for side in (0, 1):
             go(second((k & 2) + side, k & 1, from_link[k]))
+    for k in (1, 2):
+        direct(k, 1 - k // 2, from_link[k]).wait_recv()
+        go(relay(k, from_link[k]))
     for k, axis in ((0, 0), (3, 1)):
         relay(k, opposite[axis]).wait_recv()
         for side in (0, 1):
@@ -379,6 +387,8 @@
         for k in range(4):
             second(k, n, beside(k, n)).wait_recv()
             go(third(k, n))
+    for k in (0, 3):
+        direct(k, 1 - k // 2, from_link[k]).wait_recv()
     relay(1, opposite[0]).wait_recv()
     relay(2, opposite[1]).wait_recv()
     for n in range(3):
@@ -436,16 +446,16 @@
             pltpu.VMEM((ROWS, COLS), f32),
             pltpu.VMEM((1, ROWS), f32),
             pltpu.VMEM((1, COLS), f32),
-            pltpu.VMEM((NZ, 8, 256), f32),
+            pltpu.VMEM((NZ, 1, 256), f32),
             pltpu.VMEM((256, 128), f32),
             pltpu.VMEM((N * N, 2, COLS), f32),
             pltpu.VMEM((2, 2, COLS), f32),
-            pltpu.VMEM((NZ, 8, 128), f32),
+            pltpu.VMEM((NZ, 1, 128), f32),
             dma((8,)), dma((7,)), dma((7,)),
             dma((4, 3, N)), dma((4, 3, N)), dma((4, 3)), dma((4, 3)),
             dma((NZ - 1,)), dma((NZ - 1,)), dma((1,)), dma((1,)), dma((N * N - 1,)), dma((N * N - 1,)),
             dma((NZ - 1,)), dma((NZ - 1,)),
-            dma((4,)), dma((4,)), dma((4,)), dma((4,)), dma((4, 3, 2)), dma((4, 3, 2)),
+            dma((4, 2)), dma((4, 2)), dma((4,)), dma((4,)), dma((4, 3, 2)), dma((4, 3, 2)),
             pltpu.SemaphoreType.REGULAR((3,)),
         ],
         compiler_params=pltpu.CompilerParams(collective_id=0, has_side_effects=True, vmem_limit_bytes=62700000),

time: 79.9 us -> 76.1 us (0.952)
  Pallas kernels: 79.1 us -> 75.4 us
    pallas_call x1, Pallas kernels: 77 us -> 73.4 us  [per_device(): pl.pallas_call(kernel, out_shape=tuple((pltpu.VMEM(shape, kind) for shape...]
where the time goes in v3:
time: 76.1 us
  Pallas kernels  75.4 us (99%)
    pallas_call x1, Pallas kernels, per_device(): pl.pallas_call(kernel, out_shape=tuple((pltpu.VMEM(shape, kind) for shape...  73.4 us
    pallas_call x1, Pallas kernels, per_device(): pl.pallas_call(writer, out_shape=tuple((jax.ShapeDtypeStruct(shape, kind)...  2.04 us

profile of v3, /device:TPU:2, one launch (start us, length us, event | category | flops | bytes accessed | tf_op | source)
XLA Modules:
  0.0 76.1 jit_solution(14156534456777155345)
XLA Ops:
  0.6 73.4 %shard_map.84 = (bf16[16,224,512]{2,1,0:T(8,128)(2,1)S(1)}, f32[224,512]{1,0:T(8,128)S(1)}, f32[1,224]{1,0:T(1,128)S(1)}, f32[1,512]{1,0:T(1,128)S(1)}) custom-call(bf16[512,7168]{1,0:T(8,128)(2,1)} %hid.1, bf16[512,512]{1,0:T(8,128)(2,1)} %gout.1, f32[224,512]{1,0:T(8,128)} %master.1, f32[1,224]{1,0:T(1,128)} %bitcast.6, f32[1,512]{1,0:T(1,128)} %bitcast.5), custom_call_target="tpu_custom_call" | custom-call | tf_op jit(solution)/shard_map/pallas_call | solution.py:430
  74.0 2.0 %shard_map.85 = (bf16[16,224,512]{2,1,0:T(8,128)(2,1)}, f32[224,512]{1,0:T(8,128)}, f32[1,224]{1,0:T(1,128)}, f32[1,512]{1,0:T(1,128)}) custom-call(bf16[16,224,512]{2,1,0:T(8,128)(2,1)S(1)} %get-tuple-element.12.nw, f32[224,512]{1,0:T(8,128)S(1)} %get-tuple-element.13.upd, f32[1,224]{1,0:T(1,128)S(1)} %get-tuple-element.14.nrow, ...), custom_call_target="tpu_custom_call" | custom-call | tf_op jit(solution)/shard_map/pallas_call | solution.py:463

commit v4 on v3

--- a/solution.py
+++ b/solution.py
@@ -35,30 +35,31 @@
 
 
 def encode(ref, value):
-    groups = value.reshape(ROWS // G, G, H)
+    groups = value.reshape(ROWS // G, G, value.shape[1])
     peak = jnp.maximum(jnp.max(jnp.abs(groups), axis=0), 1e-30).astype(jnp.bfloat16)
     scale = TOP / peak.astype(jnp.float32)
     u = groups * scale[None]
     u2 = u * u
     u4 = u2 * u2
     u8 = u4 * u4
-    ref[pl.ds(0, ROWS), :] = (u8 * u).astype(jnp.bfloat16).reshape(ROWS, H)
+    ref[pl.ds(0, ROWS), :] = (u8 * u).astype(jnp.bfloat16).reshape(value.shape)
     ref[pl.ds(ROWS, G), :] = peak
 
 
 def decode(ref):
-    code = ref[pl.ds(0, ROWS), :].astype(jnp.float32).reshape(ROWS // G, G, H)
+    width = ref.shape[1]
+    code = ref[pl.ds(0, ROWS), :].astype(jnp.float32).reshape(ROWS // G, G, width)
     scale = ref[pl.ds(ROWS, G), :].astype(jnp.float32) * (1.0 / TOP)
     size = jnp.exp(jnp.log(jnp.maximum(jnp.abs(code), 1.2e-38)) * (1.0 / POWER))
-    return (size * jnp.where(code < 0.0, -scale[None], scale[None])).reshape(ROWS, H)
+    return (size * jnp.where(code < 0.0, -scale[None], scale[None])).reshape(ROWS, width)
 
 
 def kernel(
     hid, gout, master, rprev, cprev,
     nw, upd, nrow, ncol,
     h_own, h_par, g_own, g_par, flat, s1buf, r1buf, s2buf, r2buf, grad, mas, rp, cp,
-    rowx, tall, plane, colc, sizx,
-    ld_sem, xs_sem, xr_sem, s1s, r1s, s2s, r2s, zs, zr, cs, cr, ps, pr, ss, sr, ws, wr, bs, br, a2s, a2r, chain,
+    rowx, tall, plane, colc, sizx, mnear, rcode, rnear, dnear, down,
+    ld_sem, xs_sem, xr_sem, s1s, r1s, s2s, r2s, zs, zr, cs, cr, ps, pr, ss, sr, ws, wr, bs, br, a2s, a2r, es, er, fs, fr, chain,
 ):
     c = lax.axis_index("dp")
     s = lax.axis_index("seq")
@@ -138,10 +139,25 @@
         copy.start()
     for copy in small:
         copy.start()
+
+    def early(k, turn):
+        rows = pl.ds(turn * (ROWS // 2), ROWS // 2)
+        lanes = pl.ds((k // 2) * 2 * H, 2 * H)
+        return remote(master.at[rows, lanes], mnear.at[k, rows], es.at[k, turn], er.at[k, turn], link1[k])
+
     tell(0)
 
-    def msg1(k, kind, i):
-        return remote(s1buf.at[k, kind, i], r1buf.at[k, kind, i], s1s.at[k, kind, i], r1s.at[k, kind, i], link1[k])
+    def way(i):
+        return 1 - 2 * (i % 2)
+
+    def cols(axis):
+        return pl.ds(axis * 2 * H, 2 * H)
+
+    def msg1(axis, kind, i):
+        step = -way(i) if kind == 1 else way(i)
+        peer = at(x + step, y) if axis == 0 else at(x, y + step)
+        index = (axis, kind, i)
+        return remote(s1buf.at[index], r1buf.at[index], s1s.at[index], r1s.at[index], peer)
 
     def msg2(k, kind):
         return remote(s2buf.at[k, kind], r2buf.at[k, kind], s2s.at[k, kind], r2s.at[k, kind], link2[k])
@@ -158,9 +174,9 @@
     def part(j, v, cols):
         return flat.at[j, pl.ds(pl.multiple_of(v * ROWS, 32), ROWS), cols]
 
-    def send1(k, kind, i, value):
-        encode(s1buf.at[k, kind, i], value)
-        msg1(k, kind, i).start()
+    def send1(axis, kind, i, value):
+        encode(s1buf.at[axis, kind, i], value)
+        msg1(axis, kind, i).start()
 
     dims = (((0,), (0,)), ((), ()))
 
@@ -171,16 +187,13 @@
         return 1 if (k & 1) == 0 else -1
 
     def send_b1(j):
-        for k in (2, 3):
-            send1(k, 0, j, part(j, wrap(y + 2), own(k))[...])
+        send1(1, 0, j, part(j, wrap(y + 2), cols(1))[...])
 
     def send_b2(j):
-        for k in (2, 3):
-            send1(k, 1, j, part(j, wrap(y + ahead(k)), other(k))[...])
+        send1(1, 1, j, part(j, wrap(y - way(j)), cols(1))[...])
 
     def send_a(i, carry):
-        for k in (0, 1):
-            send1(k, 0, i, part(0, y_of(i), own(k))[...])
+        send1(0, 0, i, part(0, y_of(i), cols(0))[...])
         return carry
 
     load_g.wait()
@@ -207,15 +220,14 @@
         send_b1(j)
         send_b2(j)
 
-        for k in (0, 1):
-
-            @pl.when(j == 1 + k)
-            def _():
-                def body(i, carry):
-                    send1(k, 1, i, part(1 + k, y_of(i), other(k))[...])
-                    return carry
-
-                lax.fori_loop(0, N, body, 0)
+        @pl.when(j < 3)
+        def _():
+            def body(m, carry):
+                i = 2 * m + 2 - j
+                send1(0, 1, i, part(j, y_of(i), cols(0))[...])
+                return carry
+
+            lax.fori_loop(0, 2, body, 0)
 
         return carry
 
@@ -223,39 +235,33 @@
     told(1)
     tell(2)
 
-    def target(k, i):
+    def combine(i, carry):
+        for axis in (0, 1):
+            msg1(axis, 0, i).wait_recv()
+            mid = part(1 + i % 2, y_of(i), cols(0)) if axis == 0 else part(i, wrap(y + way(i)), cols(1))
+            send1(axis, 2, i, mid[...] + decode(r1buf.at[axis, 0, i]))
+        return carry
+
+    lax.fori_loop(0, N, combine, 0)
+
+    def mine(k, i):
+        return part(3, y_of(i), own(k)) if k < 2 else part(i, y, own(k))
+
+    def beyond(k, lanes):
         if k < 2:
-            return part(1 + k, y_of(i), own(k))
-        return part(i, wrap(y + ahead(k)), own(k))
-
-    def combine(i, carry):
-        for k in range(4):
-            msg1(k, 0, i).wait_recv()
-            send1(k, 2, i, target(k, i)[...] + decode(r1buf.at[k, 0, i]))
-        return carry
-
-    lax.fori_loop(0, N, combine, 0)
-
-    def mine(k, i):
-        if k < 2:
-            return part(3, y_of(i), own(k))
-        return part(i, y, own(k))
-
-    def beyond(k, cols):
-        if k < 2:
-            return part(3, wrap(y + ahead(k)), cols)
-        return part(1 + (k & 1), y, cols)
+            return part(3, wrap(y + ahead(k)), lanes)
+        return part(1 + (k & 1), y, lanes)
 
     def send2(k, kind, value):
         encode(s2buf.at[k, kind], value)
         msg2(k, kind).start()
 
     def settle(i, carry):
-        for k in range(4):
-            msg1(k, 1, i).wait_recv()
-            msg1(k, 2, i).wait_recv()
-        for k in range(4):
-            mine(k, i)[...] += decode(r1buf.at[k, 2, i]) + decode(r1buf.at[k ^ 1, 1, i])
+        for axis in (0, 1):
+            msg1(axis, 1, i).wait_recv()
+            msg1(axis, 2, i).wait_recv()
+            ref = part(3, y_of(i), cols(0)) if axis == 0 else part(i, y, cols(1))
+            ref[...] += decode(r1buf.at[axis, 1, i]) + decode(r1buf.at[axis, 2, i])
 
         @pl.when(i == 0)
         def _():
@@ -278,13 +284,14 @@
     for k in range(4):
         msg2(k, 1).wait_recv()
     for k in range(4):
+        grad[:, own(k)] = mine(k, 3)[...] + decode(r2buf.at[k ^ 1, 1])
+    folded = jnp.zeros((ROWS, H), jnp.float32)
+    for k in range(4):
         msg2(k, 2).wait_recv()
-    for k in range(4):
-        grad[:, own(k)] = mine(k, 3)[...] + decode(r2buf.at[k, 2]) + decode(r2buf.at[k ^ 1, 1])
-
-    g = grad[...]
-    squares = g * g + small_term
-    folded = squares[:, 0:128] + squares[:, 128:256] + squares[:, 256:384] + squares[:, 384:512]
+        final = grad[:, own(k)] + decode(r2buf.at[k, 2])
+        grad[:, own(k)] = final
+        folded = folded + (final * final + small_term)
+
     tall[pl.ds(0, ROWS), :] = folded
     tall[pl.ds(ROWS, 256 - ROWS), :] = jnp.zeros((256 - ROWS, 128), jnp.float32)
     rowx[z] = jnp.sum(tall[...].T, axis=0, keepdims=True)
@@ -301,7 +308,11 @@
         return copies
 
     pending = exchange(rowx, z, peers_z, zs, zr)
-    col_sum = jnp.sum(squares, axis=0, keepdims=True)
+    for turn in (0, 1):
+        for k in range(4):
+            early(k, turn).start()
+    g = grad[...]
+    col_sum = jnp.sum(g * g + small_term, axis=0, keepdims=True)
     for copy in small:
         copy.wait()
     arrive(pending)
@@ -325,11 +336,30 @@
     sizx[z] = short
     last = exchange(sizx, z, peers_z, ss, sr)
     raw = scaled * lax.rsqrt(new_cols)
+
+    def code(k):
+        return remote(rcode.at[k // 2], rnear.at[k], fs.at[k], fr.at[k], link1[k])
+
+    for axis in (0, 1):
+        encode(rcode.at[axis], raw[:, axis * 2 * H : (axis + 1) * 2 * H])
+        for k in (2 * axis, 2 * axis + 1):
+            code(k).start()
+    for axis in (0, 1):
+        down[:, cols(axis)] = decode(rcode.at[axis])
+    for k in (0, 2, 1, 3):
+        code(k).wait_recv()
+        dnear[k] = decode(rnear.at[k])
+        early(k, 0).wait_recv()
+        early(k, 1).wait_recv()
     pending += arrive(last)
     raw_total = jnp.sum(jnp.sum(sizx[...], axis=0), axis=1, keepdims=True)
     size = jnp.sqrt(raw_total / (FF_WIN * D))
-    update = raw * (1.0 / jnp.maximum(1.0, size))
-    nw[s] = (mas[...] - learn_rate * update).astype(jnp.bfloat16)
+    clip = 1.0 / jnp.maximum(1.0, size)
+
+    def fresh(weight, step):
+        return (weight - learn_rate * (step * clip)).astype(jnp.bfloat16)
+
+    nw[s] = fresh(mas[...], down[...])
 
     def block(px, py):
         return wrap(px) * N + wrap(py)
@@ -365,17 +395,15 @@
         copy.start()
         sends.append(copy)
 
-    for k in range(4):
-        go(direct(k, k // 2, s))
-    for k in range(4):
+    for k in (1, 2, 0, 3):
         go(direct(k, 1 - k // 2, s))
-    upd[...] = update
     for k in (0, 3, 1, 2):
-        direct(k, k // 2, from_link[k]).wait_recv()
+        nw[from_link[k], :, pair(k)] = fresh(mnear[k], dnear[k])
         if k in (0, 3):
             go(relay(k, from_link[k]))
         for side in (0, 1):
             go(second((k & 2) + side, k & 1, from_link[k]))
+    upd[...] = raw * clip
     for k in (1, 2):
         direct(k, 1 - k // 2, from_link[k]).wait_recv()
         go(relay(k, from_link[k]))
@@ -397,11 +425,15 @@
 
     for copy in sends + pending + swaps:
         copy.wait_send()
+    for k in range(4):
+        early(k, 0).wait_send()
+        early(k, 1).wait_send()
+        code(k).wait_send()
 
     def drain(i, carry):
-        for k in range(4):
+        for axis in (0, 1):
             for kind in range(3):
-                msg1(k, kind, i).wait_send()
+                msg1(axis, kind, i).wait_send()
         return carry
 
     lax.fori_loop(0, N, drain, 0)
@@ -438,8 +470,8 @@
             pltpu.VMEM((TOK, COLS), bf16),
             pltpu.VMEM((TOK, COLS), bf16),
             pltpu.VMEM((N, CHUNK, COLS), f32),
-            pltpu.VMEM((4, 3, N, MSG, H), bf16),
-            pltpu.VMEM((4, 3, N, MSG, H), bf16),
+            pltpu.VMEM((2, 3, N, MSG, 2 * H), bf16),
+            pltpu.VMEM((2, 3, N, MSG, 2 * H), bf16),
             pltpu.VMEM((4, 3, MSG, H), bf16),
             pltpu.VMEM((4, 3, MSG, H), bf16),
             pltpu.VMEM((ROWS, COLS), f32),
@@ -451,11 +483,17 @@
             pltpu.VMEM((N * N, 2, COLS), f32),
             pltpu.VMEM((2, 2, COLS), f32),
             pltpu.VMEM((NZ, 1, 128), f32),
+            pltpu.VMEM((4, ROWS, 2 * H), f32),
+            pltpu.VMEM((2, MSG, 2 * H), bf16),
+            pltpu.VMEM((4, MSG, 2 * H), bf16),
+            pltpu.VMEM((4, ROWS, 2 * H), f32),
+            pltpu.VMEM((ROWS, COLS), f32),
             dma((8,)), dma((7,)), dma((7,)),
-            dma((4, 3, N)), dma((4, 3, N)), dma((4, 3)), dma((4, 3)),
+            dma((2, 3, N)), dma((2, 3, N)), dma((4, 3)), dma((4, 3)),
             dma((NZ - 1,)), dma((NZ - 1,)), dma((1,)), dma((1,)), dma((N * N - 1,)), dma((N * N - 1,)),
             dma((NZ - 1,)), dma((NZ - 1,)),
             dma((4, 2)), dma((4, 2)), dma((4,)), dma((4,)), dma((4, 3, 2)), dma((4, 3, 2)),
+            dma((4, 2)), dma((4, 2)), dma((4,)), dma((4,)),
             pltpu.SemaphoreType.REGULAR((3,)),
         ],
         compiler_params=pltpu.CompilerParams(collective_id=0, has_side_effects=True, vmem_limit_bytes=62700000),

time: 76.1 us -> 74.7 us (0.982)
  Pallas kernels: 75.4 us -> 73.7 us
    pallas_call x1, Pallas kernels: 73.4 us -> 71.7 us  [per_device(): pl.pallas_call(kernel, out_shape=tuple((pltpu.VMEM(shape, kind) for shape...]
where the time goes in v4:
time: 74.7 us; the launch traced here: 74.3 us
  Pallas kernels  73.7 us (99%)
    pallas_call x1, Pallas kernels, per_device(): pl.pallas_call(kernel, out_shape=tuple((pltpu.VMEM(shape, kind) for shape...  71.7 us
    pallas_call x1, Pallas kernels, per_device(): pl.pallas_call(writer, out_shape=tuple((jax.ShapeDtypeStruct(shape, kind)...  2.04 us

profile of v4, /device:TPU:2, one launch (start us, length us, event | category | flops | bytes accessed | tf_op | source)
XLA Modules:
  0.0 74.3 jit_solution(2678064099066376786)
XLA Ops:
  0.6 71.7 %shard_map.84 = (bf16[16,224,512]{2,1,0:T(8,128)(2,1)S(1)}, f32[224,512]{1,0:T(8,128)S(1)}, f32[1,224]{1,0:T(1,128)S(1)}, f32[1,512]{1,0:T(1,128)S(1)}) custom-call(bf16[512,7168]{1,0:T(8,128)(2,1)} %hid.1, bf16[512,512]{1,0:T(8,128)(2,1)} %gout.1, f32[224,512]{1,0:T(8,128)} %master.1, f32[1,224]{1,0:T(1,128)} %bitcast.6, f32[1,512]{1,0:T(1,128)} %bitcast.5), custom_call_target="tpu_custom_call" | custom-call | tf_op jit(solution)/shard_map/pallas_call | solution.py:462
  72.3 2.0 %shard_map.85 = (bf16[16,224,512]{2,1,0:T(8,128)(2,1)}, f32[224,512]{1,0:T(8,128)}, f32[1,224]{1,0:T(1,128)}, f32[1,512]{1,0:T(1,128)}) custom-call(bf16[16,224,512]{2,1,0:T(8,128)(2,1)S(1)} %get-tuple-element.12.nw, f32[224,512]{1,0:T(8,128)S(1)} %get-tuple-element.13.upd, f32[1,224]{1,0:T(1,128)S(1)} %get-tuple-element.14.nrow, ...), custom_call_target="tpu_custom_call" | custom-call | tf_op jit(solution)/shard_map/pallas_call | solution.py:501

commit v5 on v4

--- a/solution.py
+++ b/solution.py
@@ -325,9 +325,19 @@
 
     colc[c, pl.ds(0, 1), :] = col_sum
     colc[c, pl.ds(1, 1), :] = jnp.sum(scaled * scaled, axis=0, keepdims=True)
-    pending += arrive(exchange(colc, c, [partner], cs, cr))
+    across = exchange(colc, c, [partner], cs, cr)
+
+    def code(k):
+        return remote(rcode.at[k // 2], rnear.at[k], fs.at[k], fr.at[k], link1[k])
+
+    for axis in (0, 1):
+        encode(rcode.at[axis], scaled[:, axis * 2 * H : (axis + 1) * 2 * H])
+    pending += arrive(across)
     plane[s] = colc[0] + colc[1]
-    pending += arrive(exchange(plane, s, peers_plane, ps, pr))
+    around = exchange(plane, s, peers_plane, ps, pr)
+    for k in range(4):
+        code(k).start()
+    pending += arrive(around)
     both = jnp.sum(plane[...], axis=0)
     new_cols = decay_rate * cp[...] + (1.0 - decay_rate) * both[0:1] / FF_WIN
     ncol[...] = new_cols
@@ -335,20 +345,18 @@
     short = ratio[:, 0:128] + ratio[:, 128:256] + ratio[:, 256:384] + ratio[:, 384:512]
     sizx[z] = short
     last = exchange(sizx, z, peers_z, ss, sr)
-    raw = scaled * lax.rsqrt(new_cols)
-
-    def code(k):
-        return remote(rcode.at[k // 2], rnear.at[k], fs.at[k], fr.at[k], link1[k])
+    col_scale = lax.rsqrt(new_cols)
+    raw = scaled * col_scale
+
+    def side_of(axis):
+        return col_scale[:, axis * 2 * H : (axis + 1) * 2 * H]
+
 
     for axis in (0, 1):
-        encode(rcode.at[axis], raw[:, axis * 2 * H : (axis + 1) * 2 * H])
-        for k in (2 * axis, 2 * axis + 1):
-            code(k).start()
-    for axis in (0, 1):
-        down[:, cols(axis)] = decode(rcode.at[axis])
+        down[:, cols(axis)] = decode(rcode.at[axis]) * side_of(axis)
     for k in (0, 2, 1, 3):
         code(k).wait_recv()
-        dnear[k] = decode(rnear.at[k])
+        dnear[k] = decode(rnear.at[k]) * side_of(k // 2)
         early(k, 0).wait_recv()
         early(k, 1).wait_recv()
     pending += arrive(last)

time: 74.7 us -> 73.4 us (0.983)
  Pallas kernels: 73.7 us -> 72.7 us
    pallas_call x1, Pallas kernels: 71.7 us -> 70.7 us  [per_device(): pl.pallas_call(kernel, out_shape=tuple((pltpu.VMEM(shape, kind) for shape...]
where the time goes in v5:
time: 73.4 us
  Pallas kernels  72.7 us (99%)
    pallas_call x1, Pallas kernels, per_device(): pl.pallas_call(kernel, out_shape=tuple((pltpu.VMEM(shape, kind) for shape...  70.7 us
    pallas_call x1, Pallas kernels, per_device(): pl.pallas_call(writer, out_shape=tuple((jax.ShapeDtypeStruct(shape, kind)...  2.04 us

profile of v5, /device:TPU:2, one launch (start us, length us, event | category | flops | bytes accessed | tf_op | source)
XLA Modules:
  0.0 73.4 jit_solution(10392296156649598957)
XLA Ops:
  0.6 70.7 %shard_map.84 = (bf16[16,224,512]{2,1,0:T(8,128)(2,1)S(1)}, f32[224,512]{1,0:T(8,128)S(1)}, f32[1,224]{1,0:T(1,128)S(1)}, f32[1,512]{1,0:T(1,128)S(1)}) custom-call(bf16[512,7168]{1,0:T(8,128)(2,1)} %hid.1, bf16[512,512]{1,0:T(8,128)(2,1)} %gout.1, f32[224,512]{1,0:T(8,128)} %master.1, f32[1,224]{1,0:T(1,128)} %bitcast.6, f32[1,512]{1,0:T(1,128)} %bitcast.5), custom_call_target="tpu_custom_call" | custom-call | tf_op jit(solution)/shard_map/pallas_call | solution.py:470
  71.3 2.0 %shard_map.85 = (bf16[16,224,512]{2,1,0:T(8,128)(2,1)}, f32[224,512]{1,0:T(8,128)}, f32[1,224]{1,0:T(1,128)}, f32[1,512]{1,0:T(1,128)}) custom-call(bf16[16,224,512]{2,1,0:T(8,128)(2,1)S(1)} %get-tuple-element.12.nw, f32[224,512]{1,0:T(8,128)S(1)} %get-tuple-element.13.upd, f32[1,224]{1,0:T(1,128)S(1)} %get-tuple-element.14.nrow, ...), custom_call_target="tpu_custom_call" | custom-call | tf_op jit(solution)/shard_map/pallas_call | solution.py:509

commit v6 on v5

--- a/solution.py
+++ b/solution.py
@@ -74,13 +74,14 @@
         return (c, wrap(px) * N + wrap(py), z)
 
     partner = (1 - c, s, z)
-    peers_plane = [at(x + d // N, y + d % N) for d in range(1, N * N)]
-    peers_z = [(c, s, lax.rem(z + d, NZ)) for d in range(1, NZ)]
+    steps = sorted(range(1, N * N), key=lambda d: -min(d // N, N - d // N) - min(d % N, N - d % N))
+    peers_plane = [at(x + d // N, y + d % N) for d in steps]
+    peers_z = [(c, s, lax.rem(z + d, NZ)) for d in (4, 3, 5, 2, 6, 1, 7)]
     right_x, left_x = at(x + 1, y), at(x - 1, y)
     right_y, left_y = at(x, y + 1), at(x, y - 1)
     link1 = [right_x, left_x, right_y, left_y]
     link2 = [right_y, left_y, right_x, left_x]
-    near = link1 + [peers_z[0], peers_z[-1]]
+    near = link1 + peers_z[-2:]
 
     barrier = pltpu.get_barrier_semaphore()
     for peer in [partner] + near:

time: 73.4 us -> 73.2 us (level)
  no operation moved by 1% of the time
where the time goes in v6:
time: 73.2 us; the launch traced here: 73.1 us
  Pallas kernels  72.5 us (99%)
    pallas_call x1, Pallas kernels, per_device(): pl.pallas_call(kernel, out_shape=tuple((pltpu.VMEM(shape, kind) for shape...  70.4 us
    pallas_call x1, Pallas kernels, per_device(): pl.pallas_call(writer, out_shape=tuple((jax.ShapeDtypeStruct(shape, kind)...  2.04 us

profile of v6, /device:TPU:2, one launch (start us, length us, event | category | flops | bytes accessed | tf_op | source)
XLA Modules:
  0.0 73.1 jit_solution(4543539372818540960)
XLA Ops:
  0.6 70.4 %shard_map.84 = (bf16[16,224,512]{2,1,0:T(8,128)(2,1)S(1)}, f32[224,512]{1,0:T(8,128)S(1)}, f32[1,224]{1,0:T(1,128)S(1)}, f32[1,512]{1,0:T(1,128)S(1)}) custom-call(bf16[512,7168]{1,0:T(8,128)(2,1)} %hid.1, bf16[512,512]{1,0:T(8,128)(2,1)} %gout.1, f32[224,512]{1,0:T(8,128)} %master.1, f32[1,224]{1,0:T(1,128)} %bitcast.6, f32[1,512]{1,0:T(1,128)} %bitcast.5), custom_call_target="tpu_custom_call" | custom-call | tf_op jit(solution)/shard_map/pallas_call | solution.py:471
  71.0 2.0 %shard_map.85 = (bf16[16,224,512]{2,1,0:T(8,128)(2,1)}, f32[224,512]{1,0:T(8,128)}, f32[1,224]{1,0:T(1,128)}, f32[1,512]{1,0:T(1,128)}) custom-call(bf16[16,224,512]{2,1,0:T(8,128)(2,1)S(1)} %get-tuple-element.12.nw, f32[224,512]{1,0:T(8,128)S(1)} %get-tuple-element.13.upd, f32[1,224]{1,0:T(1,128)S(1)} %get-tuple-element.14.nrow, ...), custom_call_target="tpu_custom_call" | custom-call | tf_op jit(solution)/shard_map/pallas_call | solution.py:510
